TPU v7x, 512 devices: a whole 4x4x16 slice. The times are simulated.
512 devices in a mesh: gx: 16 (over y_hi, x, core), gy: 32 (over z, y_lo).
Axes of the slice: x: 4, y: 4 (y_hi: 2, y_lo: 2; y = y_hi * 2 + y_lo), z: 16, core: 2. Of those that a mesh axis runs over, the one named last changes fastest.
Arguments:
- velocity: float32 [2, 1, 2048, 2048], P(None, None, 'gy', 'gx'), may hold values from -6 to 6
- weights_x: float32 [4, 4096], replicated, may hold values from -0.25 to 0.75
- weights_y: float32 [4, 4096], replicated, may hold values from -0.25 to 0.75
- acoustic: bfloat16 [4, 1, 4096, 4096], P(None, None, 'gy', 'gx'), may hold values from -6 to 6
- wall_mask: int32 [1, 4096, 4096], P(None, 'gy', 'gx'), may hold values 0 or 1
Outputs:
- advanced: bfloat16 [4, 1, 4096, 4096], P(None, None, 'gy', 'gx')
All inputs are finite; a program needn't handle non-finite values. No bound on the sum of `wall_mask` on one device may be relied on, other than what follows from the above.
Results may differ from a plain program's by a relative error of at most 0.002.
Values sent between devices are 32-bit elements; how exact they have to be, the bound alone decides.
A program may use at most 64 MiB of HBM per device.

v0:
```python
import functools
import math

import jax
import jax.numpy as jnp
import numpy as np
from jax import lax
from jax.experimental import pallas as pl
from jax.experimental.pallas import tpu as pltpu
from jax.sharding import PartitionSpec as P

F32 = jnp.float32
BF16 = jnp.bfloat16
MESH = pl.DeviceIdType.MESH
PX = 72


def two_parts(array):
    high = array.astype(BF16)
    low = (array - high.astype(np.float64)).astype(BF16)
    return np.stack([high, low])


def turn(products, modulus):
    return 2.0 * np.pi / modulus * np.mod(products, modulus).astype(np.float64)


@functools.lru_cache(maxsize=None)
def tables(ngx, ngy):
    nx, ny, ns, half = 128 * ngx, 64 * ngy, 64 // ngy, ngy // 2 + 1
    lane = np.arange(128)
    wide = np.arange(256) - 4
    place = (128 * np.arange(ngx)[:, None] + lane)[None] * np.arange(ngx)[:, None, None]
    angle = turn(place, nx)
    fx = np.concatenate([np.cos(angle), np.sin(angle)], axis=1).astype(np.float32)
    angle = turn(np.arange(64)[:, None] * lane[None], 128)
    plain = np.concatenate([np.cos(angle), np.sin(angle)], axis=1)
    first = plain.copy()
    first[0, 128:] = -((-1.0) ** lane)
    wx = np.stack([two_parts(plain), two_parts(first)])
    angle = turn(np.arange(half)[:, None] * (lane % 64)[None], ny)
    twf = np.stack([np.cos(angle), np.sin(angle)]).astype(np.float32)
    angle = turn(np.arange(64)[:, None] * np.arange(64)[None], 64)
    cos2 = np.kron(np.eye(2), np.cos(angle))
    sin2 = np.kron(np.eye(2), np.sin(angle))
    yf = two_parts(np.block([[cos2, -sin2], [sin2, cos2]]))
    angle = turn(np.arange(64)[:, None] * (lane - 4)[None], 64)
    cos2 = np.concatenate([np.cos(angle)] * 2)
    sin2 = np.concatenate([np.sin(angle)] * 2)
    yi = two_parts(np.block([[cos2, sin2], [-sin2, cos2]]))
    angle = turn(np.arange(half)[:, None] * (lane - 4)[None], ny)
    scale = np.full((half, 1), 2.0)
    scale[0] = scale[-1] = 1.0
    scale = scale / (nx * ny)
    twi = np.stack([scale * np.cos(angle), scale * np.sin(angle)]).astype(np.float32)
    k2 = np.arange(ngy)[:, None] + ngy * np.arange(ns)[None]
    angle = turn(k2[..., None] * wide, 128)
    cosine, sine = 2.0 * np.cos(angle), 2.0 * np.sin(angle)
    rows = np.zeros((ngy, 2, ns, 512))
    rows[:, 0, :, :256], rows[:, 0, :, 256:] = cosine, sine
    rows[:, 1, :, :256], rows[:, 1, :, 256:] = -sine, cosine
    packed = rows.copy()
    packed[0, 0, 0, :256], packed[0, 0, 0, 256:] = 1.0, 0.0
    packed[0, 1, 0, :256], packed[0, 1, 0, 256:] = (-1.0) ** wide, 0.0
    dx = np.stack([two_parts(rows.reshape(128, 512)), two_parts(packed.reshape(128, 512))])
    place = (128 * np.arange(ngx)[:, None] + wide)[:, None, :] * np.arange(ngx)[None, :, None]
    angle = turn(place, nx)
    cx = np.concatenate([np.cos(angle), np.sin(angle)], axis=1).astype(np.float32)
    return fx, wx, twf, yf, twi, yi, dx, cx


def rfft(values):
    count = len(values)
    if count == 1:
        return [(values[0], None)]
    even, odd = rfft(values[0::2]), rfft(values[1::2])
    if count == 2:
        return [(even[0][0] + odd[0][0], None), (even[0][0] - odd[0][0], None)]
    middle = count // 2

    def full(half, k):
        k = k % middle
        if k <= middle // 2:
            return half[k]
        real, imag = half[middle - k]
        return (real, None if imag is None else -imag)

    result = []
    for k in range(middle + 1):
        er, ei = full(even, k)
        orr, oi = full(odd, k)
        if k == 0:
            result.append((er + orr, None))
        elif k == middle:
            result.append((er - orr, None))
        elif 2 * k == middle:
            result.append((er, -orr))
        else:
            c, s = math.cos(2 * math.pi * k / count), math.sin(2 * math.pi * k / count)
            tr = c * orr + (0.0 if oi is None else s * oi)
            ti = (0.0 if oi is None else c * oi) - s * orr
            result.append((er + tr, ti if ei is None else ei + ti))
    return result


def real_sum(spectrum):
    middle = len(spectrum) - 1
    if middle == 1:
        a, b = spectrum[0][0], spectrum[1][0]
        return [a + b, a - b]
    count = 2 * middle

    def fold(values):
        folded = []
        for k in range(middle // 2 + 1):
            if 2 * k == middle:
                folded.append((values[k][0], None))
                continue
            ar, ai = values[k]
            br, bi = values[middle - k]
            if k == 0:
                folded.append((ar + br, None))
            else:
                folded.append((ar + br, ai - bi))
        return folded

    twisted = []
    for k in range(middle + 1):
        vr, vi = spectrum[k]
        if k == 0:
            twisted.append((vr, None))
        elif k == middle:
            twisted.append((-vr, None))
        elif 2 * k == middle:
            twisted.append((-vi, vr))
        else:
            c, s = math.cos(2 * math.pi * k / count), math.sin(2 * math.pi * k / count)
            twisted.append((c * vr - s * vi, c * vi + s * vr))
    even, odd = real_sum(fold(spectrum)), real_sum(fold(twisted))
    result = []
    for a, b in zip(even, odd):
        result += [a, b]
    return result


def parts(value):
    high = value.astype(BF16)
    return high, (value - high.astype(F32)).astype(BF16)


def dot(a, b):
    return jnp.dot(a, b, preferred_element_type=F32)


def dot3(left, right):
    lh, ll = left
    rh, rl = right
    return dot(lh, rh) + dot(lh, rl) + dot(ll, rh)


def dot_t(a, b):
    return lax.dot_general(a, b, (((1,), (1,)), ((), ())), preferred_element_type=F32)


def shifted(value, step):
    width = value.shape[-1]
    return pltpu.roll(value, (-step) % width, value.ndim - 1)


WEIGHTS = (0.75, -0.15, 1.0 / 60.0)


def slope_x(value):
    total = None
    for index, weight in enumerate(WEIGHTS):
        term = weight * (shifted(value, index + 1) - shifted(value, -index - 1))
        total = term if total is None else total + term
    return total


def slope_y(window, rows):
    total = None
    for index, weight in enumerate(WEIGHTS):
        k = index + 1
        term = weight * (window[8 + k : 8 + k + rows] - window[8 - k : 8 - k + rows])
        total = term if total is None else total + term
    return total


def kernel(
    ngx, ngy,
    vel, weights_x, weights_y, ac, wall, fx, wx, twf, yf, twi, yi, dx, cx,
    out,
    vg, acs, wls, wxs, wys, fxs, wxm, twfs, yfs, twis, yis, dxs, cxs,
    ext, mid, adv, pack, xsend, xrecv, ax, ay, k1, k2,
    zs, b3, r3, gs, ps, us, b4, r4, s4, sb, sg, qs,
    loc, x_send, x_recv, y_send, y_recv, h_send, h_recv, v_send, v_recv, w_send, w_recv,
):
    ns, half = 64 // ngy, ngy // 2 + 1
    rpm = max(8, 3 * ns)
    i, j = lax.axis_index("gx"), lax.axis_index("gy")
    partner = i + 1 - 2 * (i % 2)
    right, left = (i + 1) % ngx, (i + ngx - 1) % ngx
    down, up = (j + 1) % ngy, (j + ngy - 1) % ngy
    chips = ngx // 2

    barrier = pltpu.get_barrier_semaphore()

    def greet_y(k, carry):
        pl.semaphore_signal(barrier, inc=1, device_id={"gy": (j + k) % ngy}, device_id_type=MESH)
        return carry

    def greet_x(k, carry):
        pl.semaphore_signal(barrier, inc=1, device_id={"gx": (i + 2 * k) % ngx}, device_id_type=MESH)
        return carry

    lax.fori_loop(1, ngy, greet_y, 0)
    lax.fori_loop(1, chips, greet_x, 0)
    pl.semaphore_signal(barrier, inc=1, device_id={"gx": right}, device_id_type=MESH)
    pl.semaphore_signal(barrier, inc=1, device_id={"gx": left}, device_id_type=MESH)

    first = jnp.where(i == 0, 1, 0)
    sources = [
        (ac, acs), (wall, wls), (weights_x, wxs), (weights_y, wys), (vel, vg.at[i]),
        (fx.at[i], fxs), (wx.at[first], wxm), (twf, twfs), (yf, yfs), (twi, twis), (yi, yis),
        (dx, dxs), (cx.at[i], cxs),
    ]
    copies = [pltpu.make_async_copy(a, b, loc.at[n]) for n, (a, b) in enumerate(sources)]
    for copy in copies:
        copy.start()

    row = lax.broadcasted_iota(jnp.int32, (rpm, 128), 0)
    lane = lax.broadcasted_iota(jnp.int32, (rpm, 128), 1)
    field, slot = row // ns, row % ns
    wave = i + ngx * (j + ngy * slot)
    is_packed = wave == 0
    in_imag = lane >= 64
    wave_x = jnp.where(is_packed & in_imag, 64 * ngx, wave).astype(F32)

    def coefficients(q, carry):
        index = q + ngy * (lane % 64)
        wave_y = jnp.where(index >= 32 * ngy, index - 64 * ngy, index).astype(F32)
        xx, yy = wave_x * wave_x, wave_y * wave_y
        inverse = -1.0 / jnp.maximum(xx + yy, 1.0)
        k1[q] = jnp.where(field == 0, xx * inverse, jnp.where(field == 2, yy * inverse, 0.0))
        cross = (field == 1) & jnp.logical_not(is_packed) & (index != 32 * ngy)
        k2[q] = jnp.where(cross, 2.0 * wave_x * wave_y * inverse, 0.0)
        return carry

    lax.fori_loop(0, half, coefficients, 0)

    ext[:, 0:8, :] = jnp.zeros((5, 8, 384), F32)
    ext[:, 152:160, :] = jnp.zeros((5, 8, 384), F32)
    b3[...] = jnp.zeros(b3.shape, F32)
    copies[0].wait()
    copies[1].wait()
    for v in range(4):
        ext[v, 16:144, 0:256] = acs[v].astype(F32)
    ext[4, 16:144, 0:256] = 1.0 - wls[...].astype(F32)

    copies[2].wait()
    copies[3].wait()

    def tile_of(ref, column):
        return ref[:, pl.ds(pl.multiple_of(column, 128), 128)]

    narrow = lax.broadcasted_iota(jnp.int32, (4, 128), 1)
    total_x, total_y = 256 * ngx, 128 * ngy
    outer = jnp.where(
        narrow < 64,
        tile_of(wxs, (256 * i + 256) % total_x),
        tile_of(wxs, (256 * i + total_x - 128) % total_x),
    )
    tiles = [tile_of(wxs, 256 * i), tile_of(wxs, 256 * i + 128), outer]
    for t, weights in enumerate(tiles):
        fine = 128 * t + lax.broadcasted_iota(jnp.int32, (256, 128), 1)
        fine = jnp.where(fine < 320, fine, fine - 384) + 16
        coarse = lax.broadcasted_iota(jnp.int32, (256, 128), 0) - 4
        tap = coarse - (fine // 2 - 8 - 1)
        matrix = jnp.zeros((256, 128), F32)
        for s in range(4):
            matrix = matrix + jnp.where(tap == s, weights[s : s + 1, :], 0.0)
        high, low = parts(matrix)
        ax[0, :, 128 * t : 128 * t + 128] = high
        ax[1, :, 128 * t : 128 * t + 128] = low
    outer = jnp.where(
        narrow < 64,
        tile_of(wys, (128 * j + 128) % total_y),
        tile_of(wys, (128 * j + total_y - 128) % total_y),
    )
    for t, weights in enumerate([tile_of(wys, 128 * j), outer]):
        fine = 128 * t + lax.broadcasted_iota(jnp.int32, (128, 128), 1)
        fine = jnp.where(fine < 192, fine, fine - 256) + 16
        coarse = lax.broadcasted_iota(jnp.int32, (128, 128), 0) - 4
        tap = coarse - (fine // 2 - 8 - 1)
        matrix = jnp.zeros((128, 128), F32)
        for s in range(4):
            matrix = matrix + jnp.where(tap == s, weights[s : s + 1, :], 0.0)
        high, low = parts(jnp.transpose(matrix))
        ay[0, 128 * t : 128 * t + 128, :] = high
        ay[1, 128 * t : 128 * t + 128, :] = low

    pl.semaphore_wait(barrier, ngy - 1 + chips - 1 + 2)

    def gather(source, own, slots, send, recv):
        def direct(k):
            return pltpu.make_async_remote_copy(
                src_ref=source, dst_ref=slots.at[own], send_sem=send.at[k], recv_sem=recv.at[own],
                device_id={"gx": (own + 2 * k) % ngx}, device_id_type=MESH,
            )

        def to_partner(block, at, k):
            return pltpu.make_async_remote_copy(
                src_ref=block, dst_ref=slots.at[at], send_sem=send.at[k], recv_sem=recv.at[at],
                device_id={"gx": partner}, device_id_type=MESH,
            )

        def arrived(at):
            pltpu.make_async_remote_copy(
                src_ref=slots.at[at], dst_ref=slots.at[at], send_sem=send.at[0], recv_sem=recv.at[at],
                device_id={"gx": partner}, device_id_type=MESH,
            ).wait_recv()

        def start():
            def go(k, carry):
                direct(k).start()
                return carry

            lax.fori_loop(1, chips, go, 0)
            to_partner(source, own, 0).start()

        def relay():
            def step(k, carry):
                at = (own + ngx - 2 * k) % ngx
                arrived(at)
                to_partner(slots.at[at], at, chips - 1 + k).start()
                return carry

            lax.fori_loop(1, chips, step, 0)

            def rest(k, carry):
                arrived((partner + ngx - 2 * k) % ngx)
                return carry

            lax.fori_loop(0, chips, rest, 0)

        def finish():
            def step(k, carry):
                direct(k).wait_send()
                to_partner(slots.at[own], own, chips - 1 + k).wait_send()
                return carry

            lax.fori_loop(1, chips, step, 0)
            to_partner(source, own, 0).wait_send()

        return start, relay, finish

    start1, relay1, finish1 = gather(vel, i, vg, x_send, x_recv)
    start1()

    def strip(to, rows_from, rows_to, n):
        return pltpu.make_async_remote_copy(
            src_ref=ext.at[:, pl.ds(rows_from, 8), pl.ds(0, 256)],
            dst_ref=ext.at[:, pl.ds(rows_to, 8), pl.ds(0, 256)],
            send_sem=h_send.at[n], recv_sem=h_recv.at[n],
            device_id={"gy": to}, device_id_type=MESH,
        )

    go_down, go_up = strip(down, 136, 8, 0), strip(up, 16, 144, 1)
    go_down.start()
    go_up.start()
    go_down.wait()
    go_up.wait()
    ext[:, 8:16, 0:256] = jnp.where(j > 0, ext[:, 8:16, 0:256], 0.0)
    ext[:, 144:152, 0:256] = jnp.where(j < ngy - 1, ext[:, 144:152, 0:256], 0.0)

    strip_lane = lax.broadcasted_iota(jnp.int32, (144, 128), 1)
    for side in range(2):
        packed = jnp.zeros((144, 128), F32)
        for v in range(5):
            if side == 0:
                moved = pltpu.roll(ext[v, 8:152, 128:256], (8 * v - 120) % 128, 1)
            else:
                moved = pltpu.roll(ext[v, 8:152, 0:128], 8 * v, 1) if v else ext[v, 8:152, 0:128]
            packed = jnp.where((strip_lane >= 8 * v) & (strip_lane < 8 * v + 8), moved, packed)
        xsend[side] = packed

    relay1()

    def column(to, n):
        return pltpu.make_async_remote_copy(
            src_ref=xsend.at[n], dst_ref=xrecv.at[n],
            send_sem=h_send.at[2 + n], recv_sem=h_recv.at[2 + n],
            device_id={"gx": to}, device_id_type=MESH,
        )

    go_right, go_left = column(right, 0), column(left, 1)
    go_right.start()
    go_left.start()

    for n in (4, 5, 6):
        copies[n].wait()

    def combine(c, carry):
        rows = pl.ds(pl.multiple_of(8 * c, 8), 8)
        sums = [None] * 6
        for d in range(ngx):
            u, v = vg[d, 0, rows, :], vg[d, 1, rows, :]
            cosine, sine = fxs[d : d + 1, :], fxs[ngx + d : ngx + d + 1, :]
            for f, value in enumerate((u * u, u * v, v * v)):
                real, imag = value * cosine, value * sine
                sums[2 * f] = real if d == 0 else sums[2 * f] + real
                sums[2 * f + 1] = -imag if d == 0 else sums[2 * f + 1] - imag
        for f in range(3):
            zs[f, 0, rows, :] = sums[2 * f]
            zs[f, 1, rows, :] = sums[2 * f + 1]
        return carry

    lax.fori_loop(0, 8, combine, 0)
    w_high, w_low = wxm[0], wxm[1]
    for f in range(3):
        pieces = []
        for real, imag in zip(parts(zs[f, 0]), parts(zs[f, 1])):
            plain = jnp.concatenate([real, imag], axis=1)
            turned = jnp.concatenate([imag, -real], axis=1)
            both = [turned, -plain] if f == 1 else [plain, turned]
            pieces.append(jnp.concatenate(both, axis=0))
        high, low = pieces
        lines = dot_t(w_high, high) + dot_t(w_high, low) + dot_t(w_low, high)
        for s in range(ns):
            b3[pl.ds(ns * f + s, ngy, stride=rpm), :] = lines[ngy * s : ngy * s + ngy]

    def offset(m):
        step = (m + 1) // 2
        return ngy // 2 + jnp.where(m % 2 == 1, step, -step)

    def send3(k):
        to = (j + k) % ngy
        return pltpu.make_async_remote_copy(
            src_ref=b3.at[pl.ds(pl.multiple_of(to * rpm, 8), rpm), :], dst_ref=r3.at[j],
            send_sem=y_send.at[k], recv_sem=y_recv.at[j],
            device_id={"gy": to}, device_id_type=MESH,
        )

    def recv3(d):
        return pltpu.make_async_remote_copy(
            src_ref=r3.at[d], dst_ref=r3.at[d], send_sem=y_send.at[0], recv_sem=y_recv.at[d],
            device_id={"gy": d}, device_id_type=MESH,
        )

    def go3(m, carry):
        send3(offset(m)).start()
        return carry

    lax.fori_loop(0, ngy - 1, go3, 0)
    r3[j] = b3[pl.ds(pl.multiple_of(j * rpm, 8), rpm), :]

    go_right.wait()
    go_left.wait()
    for v in range(5):
        from_right = pltpu.roll(xrecv[1], (-8 * v) % 128, 1) if v else xrecv[1]
        from_left = pltpu.roll(xrecv[0], 120 - 8 * v, 1)
        from_right = jnp.where((strip_lane < 8) & (i < ngx - 1), from_right, 0.0)
        ext[v, 8:152, 256:384] = jnp.where((strip_lane >= 120) & (i > 0), from_left, from_right)

    def rates(planes, at, rows):
        here = pl.ds(at, rows)
        window = pl.ds(pl.multiple_of(at - 8, 8), rows + 16)
        b_window, p_window = planes[2, window, :], planes[3, window, :]
        b, p = b_window[8 : 8 + rows], p_window[8 : 8 + rows]
        rho, a = planes[0, here, :], planes[1, here, :]
        slope_b, slope_p = slope_y(b_window, rows), slope_y(p_window, rows)
        return (
            (rho, slope_x(a + 0.3 * rho) + slope_b),
            (a, slope_x(p + 0.3 * a)),
            (b, slope_x(0.3 * b) + slope_p),
            (p, slope_x(a + 0.3 * p) + slope_b),
        )

    def stage_one(c, carry):
        at = pl.multiple_of(8 + 8 * c, 8)
        here = pl.ds(at, 8)
        open_cells = ext[4, here, :]
        for v, (value, rate) in enumerate(rates(ext, at, 8)):
            mid[v, here, :] = open_cells * (value - 0.5 * rate)
            adv[v, here, :] = (value - 0.25 * rate)[:, 0:256]
        return carry

    lax.fori_loop(0, 18, stage_one, 0)

    def stage_two(c, carry):
        at = pl.multiple_of(16 + 8 * c, 8)
        here = pl.ds(at, 8)
        open_cells = ext[4, here, 0:256]
        for v, (value, rate) in enumerate(rates(mid, at, 8)):
            adv[v, here, :] = open_cells * (adv[v, here, :] - 0.25 * rate[:, 0:256])
        return carry

    lax.fori_loop(0, 16, stage_two, 0)

    def got3(k, carry):
        recv3((j + k) % ngy).wait_recv()
        return carry

    for n in range(7, 13):
        copies[n].wait()
    lax.fori_loop(1, ngy, got3, 0)

    spectrum = rfft([r3[d] for d in range(ngy)])
    for q, (real, imag) in enumerate(spectrum):
        rows = slice(rpm * q, rpm * q + rpm)
        cosine, sine = twfs[0, q : q + 1, :], twfs[1, q : q + 1, :]
        if imag is None:
            gs[rows, 0:128] = real * cosine
            gs[rows, 128:256] = -(real * sine)
        else:
            gs[rows, 0:128] = real * cosine + imag * sine
            gs[rows, 128:256] = imag * cosine - real * sine
    gs[...] = dot3(parts(gs[...]), (yfs[0], yfs[1]))
    corner = (row == ns) & (lane == 96) & (i == 0) & (j == 0)
    row_lane = lax.broadcasted_iota(jnp.int32, (ns, 128), 1)
    for q in range(half):
        real, imag = gs[rpm * q : rpm * q + rpm, 0:128], gs[rpm * q : rpm * q + rpm, 128:256]
        total_real = k1[q] * real - k2[q] * imag
        total_imag = k1[q] * imag + k2[q] * real
        if q == 0:
            total_real = total_real - jnp.where(corner, pltpu.roll(real, 64, 1), 0.0)
            total_imag = total_imag - jnp.where(corner, pltpu.roll(imag, 64, 1), 0.0)
        for n, total in enumerate((total_real, total_imag)):
            value = total[0:ns] + total[ns : 2 * ns] + total[2 * ns : 3 * ns]
            lanes = slice(128 * n, 128 * n + 128)
            at = 2 * ns * q
            ps[at : at + ns, lanes] = jnp.where(row_lane < 64, value, 0.0)
            ps[at + ns : at + 2 * ns, lanes] = jnp.where(row_lane < 64, 0.0, value)
    us[...] = dot3(parts(ps[...]), (yis[0], yis[1]))
    terms = []
    for q in range(half):
        rows = slice(2 * ns * q, 2 * ns * q + 2 * ns)
        real, imag = us[rows, 0:128], us[rows, 128:256]
        cosine, sine = twis[0, q : q + 1, :], twis[1, q : q + 1, :]
        turned_real = real * cosine - imag * sine
        if q in (0, half - 1):
            terms.append((turned_real, None))
        else:
            terms.append((turned_real, real * sine + imag * cosine))
    for d, value in enumerate(real_sum(terms)):
        b4[d] = value

    def send4(k):
        to = (j + k) % ngy
        return pltpu.make_async_remote_copy(
            src_ref=b4.at[to], dst_ref=r4.at[j], send_sem=v_send.at[k], recv_sem=v_recv.at[j],
            device_id={"gy": to}, device_id_type=MESH,
        )

    def recv4(d):
        return pltpu.make_async_remote_copy(
            src_ref=r4.at[d], dst_ref=r4.at[d], send_sem=v_send.at[0], recv_sem=v_recv.at[d],
            device_id={"gy": d}, device_id_type=MESH,
        )

    def go4(m, carry):
        send4(offset(m)).start()
        return carry

    def got4(k, carry):
        recv4((j + k) % ngy).wait_recv()
        return carry

    lax.fori_loop(0, ngy - 1, go4, 0)
    r4[j] = b4[j]
    lax.fori_loop(1, ngy, got4, 0)
    for g in range(ngy):
        s4[2 * ns * g : 2 * ns * g + 2 * ns, :] = r4[g]
    sb[...] = jnp.transpose(s4[...])[0:PX]
    start2, relay2, finish2 = gather(sb, i, sg, w_send, w_recv)
    start2()
    sg[i] = sb[...]
    relay2()

    pressure = jnp.zeros((PX, 256), F32)
    blocks = [(0, 1, 1)] + [(a, min(a + 5, ngx), 0) for a in range(1, ngx, 5)]
    for begin, end, variant in blocks:
        lines = sg[begin:end].reshape((end - begin) * PX, 128)
        mixed = dot3(parts(lines), (dxs[variant, 0], dxs[variant, 1]))
        for n in range(begin, end):
            rows = slice((n - begin) * PX, (n - begin + 1) * PX)
            cosine, sine = cxs[n : n + 1, :], cxs[ngx + n : ngx + n + 1, :]
            pressure = pressure + (mixed[rows, 0:256] * cosine - mixed[rows, 256:512] * sine)

    along = dot3(parts(pressure), (ax[0], ax[1]))
    along = jnp.concatenate([along, jnp.zeros((128 - PX, 384), F32)], axis=0)
    source = dot3((ay[0], ay[1]), parts(along))
    qs[16:152, :] = 0.5 * ext[4, 16:152, :] * source[0:136]
    qs[8:16, :] = 0.5 * ext[4, 8:16, :] * source[248:256]
    qs[0:8, :] = jnp.zeros((8, 384), F32)
    qs[152:160, :] = jnp.zeros((8, 384), F32)

    def last(c, carry):
        at = pl.multiple_of(16 + 16 * c, 16)
        here = pl.ds(at, 16)
        there = pl.ds(pl.multiple_of(16 * c, 16), 16)
        window = qs[pl.ds(pl.multiple_of(at - 8, 8), 32), :]
        half_source = window[8:24]
        quarter = 0.25 * ext[4, here, 0:256]
        change_x = quarter * slope_x(half_source)[:, 0:256]
        change_y = quarter * slope_y(window, 16)[:, 0:256]
        out[0, there, :] = adv[0, here, :].astype(BF16)
        out[1, there, :] = (adv[1, here, :] - change_x).astype(BF16)
        out[2, there, :] = (adv[2, here, :] - change_y).astype(BF16)
        out[3, there, :] = (adv[3, here, :] + half_source[:, 0:256] - 0.3 * change_x).astype(BF16)
        return carry

    lax.fori_loop(0, 8, last, 0)

    finish1()
    finish2()

    def left3(k, carry):
        send3(k).wait_send()
        return carry

    def left4(k, carry):
        send4(k).wait_send()
        return carry

    lax.fori_loop(1, ngy, left3, 0)
    lax.fori_loop(1, ngy, left4, 0)


def solution(mesh):
    ngx, ngy = mesh.shape["gx"], mesh.shape["gy"]
    ns, half = 64 // ngy, ngy // 2 + 1
    rpm = max(8, 3 * ns)
    consts = tables(ngx, ngy)

    def shards(velocity, weights_x, weights_y, acoustic, wall_mask):
        vel = velocity.reshape(2, 64, 128)
        ac = acoustic.reshape(4, 128, 256)
        wall = wall_mask.reshape(128, 256)
        fx, wx, twf, yf, twi, yi, dx, cx = [jnp.asarray(c) for c in consts]
        anywhere = pl.BlockSpec(memory_space=pl.ANY)
        vmem = pltpu.VMEM
        dma = pltpu.SemaphoreType.DMA
        scratch = [
            vmem((ngx, 2, 64, 128), F32),
            vmem((4, 128, 256), BF16),
            vmem((128, 256), jnp.int32),
            vmem((4, 256 * ngx), F32),
            vmem((4, 128 * ngy), F32),
            vmem(fx.shape[1:], F32),
            vmem(wx.shape[1:], BF16),
            vmem(twf.shape, F32),
            vmem(yf.shape, BF16),
            vmem(twi.shape, F32),
            vmem(yi.shape, BF16),
            vmem(dx.shape, BF16),
            vmem(cx.shape[1:], F32),
            vmem((5, 160, 384), F32),
            vmem((4, 160, 384), F32),
            vmem((4, 160, 256), F32),
            vmem((8, 128), F32),
            vmem((2, 144, 128), F32),
            vmem((2, 144, 128), F32),
            vmem((2, 256, 384), BF16),
            vmem((2, 256, 128), BF16),
            vmem((half, rpm, 128), F32),
            vmem((half, rpm, 128), F32),
            vmem((3, 2, 64, 128), F32),
            vmem((ngy * rpm, 128), F32),
            vmem((ngy, rpm, 128), F32),
            vmem((half * rpm, 256), F32),
            vmem((half * 2 * ns, 256), F32),
            vmem((half * 2 * ns, 256), F32),
            vmem((ngy, 2 * ns, 128), F32),
            vmem((ngy, 2 * ns, 128), F32),
            vmem((128, 128), F32),
            vmem((PX, 128), F32),
            vmem((ngx, PX, 128), F32),
            vmem((160, 384), F32),
            dma((13,)),
            dma((ngx,)), dma((ngx,)),
            dma((ngy,)), dma((ngy,)),
            dma((4,)), dma((4,)),
            dma((ngy,)), dma((ngy,)),
            dma((ngx,)), dma((ngx,)),
        ]
        result = pl.pallas_call(
            functools.partial(kernel, ngx, ngy),
            out_shape=jax.ShapeDtypeStruct((4, 128, 256), BF16),
            in_specs=[anywhere] * 13,
            out_specs=pl.BlockSpec(memory_space=pltpu.VMEM),
            scratch_shapes=scratch,
            compiler_params=pltpu.CompilerParams(
                collective_id=0, has_side_effects=True, vmem_limit_bytes=40 * 1024 * 1024
            ),
            name="poisson_step",
        )(vel, weights_x, weights_y, ac, wall, fx, wx, twf, yf, twi, yi, dx, cx)
        return result.reshape(4, 1, 128, 256)

    in_specs = (P(None, None, "gy", "gx"), P(), P(), P(None, None, "gy", "gx"), P(None, "gy", "gx"))
    return jax.shard_map(
        shards, mesh=mesh, in_specs=in_specs, out_specs=P(None, None, "gy", "gx"), check_vma=False
    )
```

profile of v0, /device:TPU:1, one launch (start us, length us, event | category | flops | bytes accessed | tf_op | source)
XLA Modules:
  0.0 71.5 jit_solution(14917499213766850486)
XLA Ops:
  0.0 0.0 copy-start
  0.0 1.0 %copy-done = f32[16,32,256]{2,1,0:T(8,128)S(1)} copy-done((f32[16,32,256]{2,1,0:T(8,128)S(1)}, f32[16,32,256]{2,1,0:T(8,128)}, u32[]{:S(2)}) %copy-start) | copy-done | bytes 524312
  1.0 0.0 copy-start.1
  1.0 1.0 %copy-done.1 = bf16[2,2,128,512]{3,2,1,0:T(8,128)(2,1)S(1)} copy-done((bf16[2,2,128,512]{3,2,1,0:T(8,128)(2,1)S(1)}, bf16[2,2,128,512]{3,2,1,0:T(8,128)(2,1)}, u32[]{:S(2)}) %copy-start.1) | copy-done | bytes 524312
  2.1 0.0 copy-start.2
  2.1 0.9 %copy-done.2 = bf16[4,1,128,256]{3,2,1,0:T(8,128)(2,1)S(1)} copy-done((bf16[4,1,128,256]{3,2,1,0:T(8,128)(2,1)S(1)}, bf16[4,1,128,256]{3,2,1,0:T(8,128)(2,1)}, u32[]{:S(2)}) %copy-start.2) | copy-done | bytes 262168
  3.0 0.0 copy-start.3
  3.0 0.9 %copy-done.3 = bf16[2,256,256]{2,1,0:T(8,128)(2,1)S(1)} copy-done((bf16[2,256,256]{2,1,0:T(8,128)(2,1)S(1)}, bf16[2,256,256]{2,1,0:T(8,128)(2,1)}, u32[]{:S(2)}) %copy-start.3) | copy-done | bytes 262168
  4.0 0.0 copy-start.4
  4.0 0.9 %copy-done.4 = bf16[2,256,256]{2,1,0:T(8,128)(2,1)S(1)} copy-done((bf16[2,256,256]{2,1,0:T(8,128)(2,1)S(1)}, bf16[2,256,256]{2,1,0:T(8,128)(2,1)}, u32[]{:S(2)}) %copy-start.4) | copy-done | bytes 262168
  4.9 0.0 copy-start.5
  4.9 0.9 %copy-done.5 = f32[16,32,128]{2,1,0:T(8,128)S(1)} copy-done((f32[16,32,128]{2,1,0:T(8,128)S(1)}, f32[16,32,128]{2,1,0:T(8,128)}, u32[]{:S(2)}) %copy-start.5) | copy-done | bytes 262168
  5.9 0.0 copy-start.6
  5.9 0.9 %copy-done.6 = s32[1,128,256]{2,1,0:T(8,128)S(1)} copy-done((s32[1,128,256]{2,1,0:T(8,128)S(1)}, s32[1,128,256]{2,1,0:T(8,128)}, u32[]{:S(2)}) %copy-start.6) | copy-done | bytes 131096
  6.8 0.0 copy-start.7
  6.8 0.9 %copy-done.7 = bf16[2,2,64,256]{3,2,1,0:T(8,128)(2,1)S(1)} copy-done((bf16[2,2,64,256]{3,2,1,0:T(8,128)(2,1)S(1)}, bf16[2,2,64,256]{3,2,1,0:T(8,128)(2,1)}, u32[]{:S(2)}) %copy-start.7) | copy-done | bytes 131096
  7.7 0.0 copy-start.8
  7.7 0.8 %copy-done.8 = f32[2,1,64,128]{3,2,1,0:T(8,128)S(1)} copy-done((f32[2,1,64,128]{3,2,1,0:T(8,128)S(1)}, f32[2,1,64,128]{3,2,1,0:T(8,128)}, u32[]{:S(2)}) %copy-start.8) | copy-done | bytes 65560
  8.5 0.0 copy-start.9
  8.5 0.8 %copy-done.9 = f32[4,4096]{1,0:T(4,128)S(1)} copy-done((f32[4,4096]{1,0:T(4,128)S(1)}, f32[4,4096]{1,0:T(4,128)}, u32[]{:S(2)}) %copy-start.9) | copy-done | bytes 65560
  9.4 0.0 copy-start.10
  9.4 0.8 %copy-done.10 = f32[4,4096]{1,0:T(4,128)S(1)} copy-done((f32[4,4096]{1,0:T(4,128)S(1)}, f32[4,4096]{1,0:T(4,128)}, u32[]{:S(2)}) %copy-start.10) | copy-done | bytes 65560
  10.2 0.0 copy-start.11
  10.2 0.7 %copy-done.11 = f32[2,17,128]{2,1,0:T(8,128)S(1)} copy-done((f32[2,17,128]{2,1,0:T(8,128)S(1)}, f32[2,17,128]{2,1,0:T(8,128)}, u32[]{:S(2)}) %copy-start.11) | copy-done | bytes 17432
  11.0 0.0 copy-start.12
  11.0 0.7 %copy-done.12 = f32[2,17,128]{2,1,0:T(8,128)S(1)} copy-done((f32[2,17,128]{2,1,0:T(8,128)S(1)}, f32[2,17,128]{2,1,0:T(8,128)}, u32[]{:S(2)}) %copy-start.12) | copy-done | bytes 17432
  11.7 59.1 %poisson_step.1 = bf16[4,128,256]{2,1,0:T(8,128)(2,1)S(1)} custom-call(f32[2,64,128]{2,1,0:T(8,128)S(1)} %bitcast.9, f32[4,4096]{1,0:T(4,128)S(1)} %copy-done.9, f32[4,4096]{1,0:T(4,128)S(1)} %copy-done.10, bf16[4,128,256]{2,1,0:T(8,128)(2,1)S(1)} %bitcast.7, s32[128,256]{1,0:T(8,128)S(1)} %bitcast.8, f32[16,32,128]{2,1,0:T(8,128)S(1)} %copy-done.5, ...), custom_call_target="tpu_custom_call" | custom-call | tf_op jit(solution)/shard_map/poisson_step/pallas_call | solution.py:688
  70.8 0.7 copy.16
Async XLA Ops:
  0.0 1.0 %copy-start = (f32[16,32,256]{2,1,0:T(8,128)S(1)}, f32[16,32,256]{2,1,0:T(8,128)}, u32[]{:S(2)}) copy-start(f32[16,32,256]{2,1,0:T(8,128)} %constant.23.clone.cx) | copy-start | bytes 1572868
  1.0 1.0 %copy-start.1 = (bf16[2,2,128,512]{3,2,1,0:T(8,128)(2,1)S(1)}, bf16[2,2,128,512]{3,2,1,0:T(8,128)(2,1)}, u32[]{:S(2)}) copy-start(bf16[2,2,128,512]{3,2,1,0:T(8,128)(2,1)} %constant.22.clone.dx) | copy-start | bytes 1572868
  2.1 0.9 %copy-start.2 = (bf16[4,1,128,256]{3,2,1,0:T(8,128)(2,1)S(1)}, bf16[4,1,128,256]{3,2,1,0:T(8,128)(2,1)}, u32[]{:S(2)}) copy-start(bf16[4,1,128,256]{3,2,1,0:T(8,128)(2,1)} %param.16) | copy-start | bytes 786436
  3.0 0.9 %copy-start.3 = (bf16[2,256,256]{2,1,0:T(8,128)(2,1)S(1)}, bf16[2,256,256]{2,1,0:T(8,128)(2,1)}, u32[]{:S(2)}) copy-start(bf16[2,256,256]{2,1,0:T(8,128)(2,1)} %constant.21.clone.yi) | copy-start | bytes 786436
  4.0 0.9 %copy-start.4 = (bf16[2,256,256]{2,1,0:T(8,128)(2,1)S(1)}, bf16[2,256,256]{2,1,0:T(8,128)(2,1)}, u32[]{:S(2)}) copy-start(bf16[2,256,256]{2,1,0:T(8,128)(2,1)} %constant.19.clone.yf) | copy-start | bytes 786436
  4.9 0.9 %copy-start.5 = (f32[16,32,128]{2,1,0:T(8,128)S(1)}, f32[16,32,128]{2,1,0:T(8,128)}, u32[]{:S(2)}) copy-start(f32[16,32,128]{2,1,0:T(8,128)} %constant.16.clone.fx) | copy-start | bytes 786436
  5.9 0.9 %copy-start.6 = (s32[1,128,256]{2,1,0:T(8,128)S(1)}, s32[1,128,256]{2,1,0:T(8,128)}, u32[]{:S(2)}) copy-start(s32[1,128,256]{2,1,0:T(8,128)} %param.17) | copy-start | bytes 393220
  6.8 0.9 %copy-start.7 = (bf16[2,2,64,256]{3,2,1,0:T(8,128)(2,1)S(1)}, bf16[2,2,64,256]{3,2,1,0:T(8,128)(2,1)}, u32[]{:S(2)}) copy-start(bf16[2,2,64,256]{3,2,1,0:T(8,128)(2,1)} %constant.17.clone.wx) | copy-start | bytes 393220
  7.7 0.8 %copy-start.8 = (f32[2,1,64,128]{3,2,1,0:T(8,128)S(1)}, f32[2,1,64,128]{3,2,1,0:T(8,128)}, u32[]{:S(2)}) copy-start(f32[2,1,64,128]{3,2,1,0:T(8,128)} %param.13) | copy-start | bytes 196612
  8.5 0.8 %copy-start.9 = (f32[4,4096]{1,0:T(4,128)S(1)}, f32[4,4096]{1,0:T(4,128)}, u32[]{:S(2)}) copy-start(f32[4,4096]{1,0:T(4,128)} %weights_x.1) | copy-start | bytes 196612
  9.4 0.8 %copy-start.10 = (f32[4,4096]{1,0:T(4,128)S(1)}, f32[4,4096]{1,0:T(4,128)}, u32[]{:S(2)}) copy-start(f32[4,4096]{1,0:T(4,128)} %weights_y.1) | copy-start | bytes 196612
  10.2 0.7 %copy-start.11 = (f32[2,17,128]{2,1,0:T(8,128)S(1)}, f32[2,17,128]{2,1,0:T(8,128)}, u32[]{:S(2)}) copy-start(f32[2,17,128]{2,1,0:T(8,128)} %constant.20.clone.twi) | copy-start | bytes 52228
  11.0 0.7 %copy-start.12 = (f32[2,17,128]{2,1,0:T(8,128)S(1)}, f32[2,17,128]{2,1,0:T(8,128)}, u32[]{:S(2)}) copy-start(f32[2,17,128]{2,1,0:T(8,128)} %constant.18.clone.twf) | copy-start | bytes 52228
where the time goes:
time: 72.1 us; the launch traced here: 71.5 us
  Pallas kernels  59.1 us (82%)
  local copies, waits for them, and re-layouts  12.4 us (17%)
    pallas_call x1, Pallas kernels, shards(): pl.pallas_call(functools.partial(kernel, ngx, ngy), out_shape=jax.ShapeDt...  59.1 us
    unnamed x27, local copies, waits for them, and re-layouts  12.4 us

commit v1 on v0

--- a/solution.py
+++ b/solution.py
@@ -192,9 +192,9 @@
     vel, weights_x, weights_y, ac, wall, fx, wx, twf, yf, twi, yi, dx, cx,
     out,
     vg, acs, wls, wxs, wys, fxs, wxm, twfs, yfs, twis, yis, dxs, cxs,
-    ext, mid, adv, pack, xsend, xrecv, ax, ay, k1, k2,
+    ext, mid, adv, xsend, xrecv, ax, ay, k1, k2,
     zs, b3, r3, gs, ps, us, b4, r4, s4, sb, sg, qs,
-    loc, x_send, x_recv, y_send, y_recv, h_send, h_recv, v_send, v_recv, w_send, w_recv,
+    loc, x_send, x_recv, y_send, y_recv, h_send, h_recv, v_send, v_recv, w_send, w_recv, token,
 ):
     ns, half = 64 // ngy, ngy // 2 + 1
     rpm = max(8, 3 * ns)
@@ -205,16 +205,20 @@
     chips = ngx // 2
 
     barrier = pltpu.get_barrier_semaphore()
+    near = ngy // 4
 
     def greet_y(k, carry):
         pl.semaphore_signal(barrier, inc=1, device_id={"gy": (j + k) % ngy}, device_id_type=MESH)
+        pl.semaphore_signal(
+            barrier, inc=1, device_id={"gy": (j + ngy - k) % ngy}, device_id_type=MESH
+        )
         return carry
 
     def greet_x(k, carry):
         pl.semaphore_signal(barrier, inc=1, device_id={"gx": (i + 2 * k) % ngx}, device_id_type=MESH)
         return carry
 
-    lax.fori_loop(1, ngy, greet_y, 0)
+    lax.fori_loop(1, near + 1, greet_y, 0)
     lax.fori_loop(1, chips, greet_x, 0)
     pl.semaphore_signal(barrier, inc=1, device_id={"gx": right}, device_id_type=MESH)
     pl.semaphore_signal(barrier, inc=1, device_id={"gx": left}, device_id_type=MESH)
@@ -229,6 +233,173 @@
     for copy in copies:
         copy.start()
 
+    pl.semaphore_wait(barrier, 2 * near + chips - 1 + 2)
+
+    def gather(source, own, slots, send, recv):
+        def direct(k):
+            return pltpu.make_async_remote_copy(
+                src_ref=source, dst_ref=slots.at[own], send_sem=send.at[k], recv_sem=recv.at[own],
+                device_id={"gx": (own + 2 * k) % ngx}, device_id_type=MESH,
+            )
+
+        def to_partner(block, at, k):
+            return pltpu.make_async_remote_copy(
+                src_ref=block, dst_ref=slots.at[at], send_sem=send.at[k], recv_sem=recv.at[at],
+                device_id={"gx": partner}, device_id_type=MESH,
+            )
+
+        def arrived(at):
+            pltpu.make_async_remote_copy(
+                src_ref=slots.at[at], dst_ref=slots.at[at], send_sem=send.at[0], recv_sem=recv.at[at],
+                device_id={"gx": partner}, device_id_type=MESH,
+            ).wait_recv()
+
+        def start():
+            def go(k, carry):
+                direct(k).start()
+                return carry
+
+            lax.fori_loop(1, chips, go, 0)
+            to_partner(source, own, 0).start()
+
+        def relay():
+            def step(k, carry):
+                at = (own + ngx - 2 * k) % ngx
+                arrived(at)
+                to_partner(slots.at[at], at, chips - 1 + k).start()
+                return carry
+
+            lax.fori_loop(1, chips, step, 0)
+
+            def rest(k, carry):
+                arrived((partner + ngx - 2 * k) % ngx)
+                return carry
+
+            lax.fori_loop(0, chips, rest, 0)
+
+        def finish():
+            def step(k, carry):
+                direct(k).wait_send()
+                to_partner(slots.at[own], own, chips - 1 + k).wait_send()
+                return carry
+
+            lax.fori_loop(1, chips, step, 0)
+            to_partner(source, own, 0).wait_send()
+
+        return start, relay, finish
+
+    start1, relay1, finish1 = gather(vel, i, vg, x_send, x_recv)
+    start1()
+    pl.semaphore_signal(token, inc=1, device_id={"gy": (j + near) % ngy}, device_id_type=MESH)
+    pl.semaphore_signal(token, inc=1, device_id={"gy": (j + ngy - near) % ngy}, device_id_type=MESH)
+    b3[...] = jnp.zeros(b3.shape, F32)
+    ext[:, 0:8, :] = jnp.zeros((5, 8, 384), F32)
+    ext[:, 152:160, :] = jnp.zeros((5, 8, 384), F32)
+    copies[0].wait()
+    copies[1].wait()
+    for v in range(4):
+        ext[v, 16:144, 0:256] = acs[v].astype(F32)
+    ext[4, 16:144, 0:256] = 1.0 - wls[...].astype(F32)
+
+
+    def strip(to, rows_from, rows_to, n):
+        return pltpu.make_async_remote_copy(
+            src_ref=ext.at[:, pl.ds(rows_from, 8), pl.ds(0, 256)],
+            dst_ref=ext.at[:, pl.ds(rows_to, 8), pl.ds(0, 256)],
+            send_sem=h_send.at[n], recv_sem=h_recv.at[n],
+            device_id={"gy": to}, device_id_type=MESH,
+        )
+
+    go_down, go_up = strip(down, 136, 8, 0), strip(up, 16, 144, 1)
+    go_down.start()
+    go_up.start()
+    relay1()
+
+    for n in (4, 5, 6):
+        copies[n].wait()
+
+    def combine(c, carry):
+        rows = pl.ds(pl.multiple_of(8 * c, 8), 8)
+        sums = [None] * 6
+        for d in range(ngx):
+            u, v = vg[d, 0, rows, :], vg[d, 1, rows, :]
+            cosine, sine = fxs[d : d + 1, :], fxs[ngx + d : ngx + d + 1, :]
+            for f, value in enumerate((u * u, u * v, v * v)):
+                real, imag = value * cosine, value * sine
+                sums[2 * f] = real if d == 0 else sums[2 * f] + real
+                sums[2 * f + 1] = -imag if d == 0 else sums[2 * f + 1] - imag
+        for f in range(3):
+            zs[f, 0, rows, :] = sums[2 * f]
+            zs[f, 1, rows, :] = sums[2 * f + 1]
+        return carry
+
+    lax.fori_loop(0, 8, combine, 0)
+    w_high, w_low = wxm[0], wxm[1]
+    for f in range(3):
+        pieces = []
+        for real, imag in zip(parts(zs[f, 0]), parts(zs[f, 1])):
+            plain = jnp.concatenate([real, imag], axis=1)
+            turned = jnp.concatenate([imag, -real], axis=1)
+            both = [turned, -plain] if f == 1 else [plain, turned]
+            pieces.append(jnp.concatenate(both, axis=0))
+        high, low = pieces
+        lines = dot_t(w_high, high) + dot_t(w_high, low) + dot_t(w_low, high)
+        for s in range(ns):
+            b3[pl.ds(ns * f + s, ngy, stride=rpm), :] = lines[ngy * s : ngy * s + ngy]
+
+    def offset(m):
+        step = (m + 1) // 2
+        return ngy // 2 + jnp.where(m % 2 == 1, step, -step)
+
+    def send3(k):
+        to = (j + k) % ngy
+        return pltpu.make_async_remote_copy(
+            src_ref=b3.at[pl.ds(pl.multiple_of(to * rpm, 8), rpm), :], dst_ref=r3.at[j],
+            send_sem=y_send.at[k], recv_sem=y_recv.at[j],
+            device_id={"gy": to}, device_id_type=MESH,
+        )
+
+    def recv3(d):
+        return pltpu.make_async_remote_copy(
+            src_ref=r3.at[d], dst_ref=r3.at[d], send_sem=y_send.at[0], recv_sem=y_recv.at[d],
+            device_id={"gy": d}, device_id_type=MESH,
+        )
+
+    def go3(m, carry):
+        send3(offset(m)).start()
+        return carry
+
+    pl.semaphore_wait(token, 2)
+    lax.fori_loop(0, ngy - 1, go3, 0)
+    r3[j] = b3[pl.ds(pl.multiple_of(j * rpm, 8), rpm), :]
+
+    go_down.wait()
+    go_up.wait()
+    ext[:, 8:16, 0:256] = jnp.where(j > 0, ext[:, 8:16, 0:256], 0.0)
+    ext[:, 144:152, 0:256] = jnp.where(j < ngy - 1, ext[:, 144:152, 0:256], 0.0)
+
+    strip_lane = lax.broadcasted_iota(jnp.int32, (144, 128), 1)
+    for side in range(2):
+        packed = jnp.zeros((144, 128), F32)
+        for v in range(5):
+            if side == 0:
+                moved = pltpu.roll(ext[v, 8:152, 128:256], (8 * v - 120) % 128, 1)
+            else:
+                moved = pltpu.roll(ext[v, 8:152, 0:128], 8 * v, 1) if v else ext[v, 8:152, 0:128]
+            packed = jnp.where((strip_lane >= 8 * v) & (strip_lane < 8 * v + 8), moved, packed)
+        xsend[side] = packed
+
+    def column(to, n):
+        return pltpu.make_async_remote_copy(
+            src_ref=xsend.at[n], dst_ref=xrecv.at[n],
+            send_sem=h_send.at[2 + n], recv_sem=h_recv.at[2 + n],
+            device_id={"gx": to}, device_id_type=MESH,
+        )
+
+    go_right, go_left = column(right, 0), column(left, 1)
+    go_right.start()
+    go_left.start()
+
     row = lax.broadcasted_iota(jnp.int32, (rpm, 128), 0)
     lane = lax.broadcasted_iota(jnp.int32, (rpm, 128), 1)
     field, slot = row // ns, row % ns
@@ -248,15 +419,6 @@
         return carry
 
     lax.fori_loop(0, half, coefficients, 0)
-
-    ext[:, 0:8, :] = jnp.zeros((5, 8, 384), F32)
-    ext[:, 152:160, :] = jnp.zeros((5, 8, 384), F32)
-    b3[...] = jnp.zeros(b3.shape, F32)
-    copies[0].wait()
-    copies[1].wait()
-    for v in range(4):
-        ext[v, 16:144, 0:256] = acs[v].astype(F32)
-    ext[4, 16:144, 0:256] = 1.0 - wls[...].astype(F32)
 
     copies[2].wait()
     copies[3].wait()
@@ -300,161 +462,6 @@
         ay[0, 128 * t : 128 * t + 128, :] = high
         ay[1, 128 * t : 128 * t + 128, :] = low
 
-    pl.semaphore_wait(barrier, ngy - 1 + chips - 1 + 2)
-
-    def gather(source, own, slots, send, recv):
-        def direct(k):
-            return pltpu.make_async_remote_copy(
-                src_ref=source, dst_ref=slots.at[own], send_sem=send.at[k], recv_sem=recv.at[own],
-                device_id={"gx": (own + 2 * k) % ngx}, device_id_type=MESH,
-            )
-
-        def to_partner(block, at, k):
-            return pltpu.make_async_remote_copy(
-                src_ref=block, dst_ref=slots.at[at], send_sem=send.at[k], recv_sem=recv.at[at],
-                device_id={"gx": partner}, device_id_type=MESH,
-            )
-
-        def arrived(at):
-            pltpu.make_async_remote_copy(
-                src_ref=slots.at[at], dst_ref=slots.at[at], send_sem=send.at[0], recv_sem=recv.at[at],
-                device_id={"gx": partner}, device_id_type=MESH,
-            ).wait_recv()
-
-        def start():
-            def go(k, carry):
-                direct(k).start()
-                return carry
-
-            lax.fori_loop(1, chips, go, 0)
-            to_partner(source, own, 0).start()
-
-        def relay():
-            def step(k, carry):
-                at = (own + ngx - 2 * k) % ngx
-                arrived(at)
-                to_partner(slots.at[at], at, chips - 1 + k).start()
-                return carry
-
-            lax.fori_loop(1, chips, step, 0)
-
-            def rest(k, carry):
-                arrived((partner + ngx - 2 * k) % ngx)
-                return carry
-
-            lax.fori_loop(0, chips, rest, 0)
-
-        def finish():
-            def step(k, carry):
-                direct(k).wait_send()
-                to_partner(slots.at[own], own, chips - 1 + k).wait_send()
-                return carry
-
-            lax.fori_loop(1, chips, step, 0)
-            to_partner(source, own, 0).wait_send()
-
-        return start, relay, finish
-
-    start1, relay1, finish1 = gather(vel, i, vg, x_send, x_recv)
-    start1()
-
-    def strip(to, rows_from, rows_to, n):
-        return pltpu.make_async_remote_copy(
-            src_ref=ext.at[:, pl.ds(rows_from, 8), pl.ds(0, 256)],
-            dst_ref=ext.at[:, pl.ds(rows_to, 8), pl.ds(0, 256)],
-            send_sem=h_send.at[n], recv_sem=h_recv.at[n],
-            device_id={"gy": to}, device_id_type=MESH,
-        )
-
-    go_down, go_up = strip(down, 136, 8, 0), strip(up, 16, 144, 1)
-    go_down.start()
-    go_up.start()
-    go_down.wait()
-    go_up.wait()
-    ext[:, 8:16, 0:256] = jnp.where(j > 0, ext[:, 8:16, 0:256], 0.0)
-    ext[:, 144:152, 0:256] = jnp.where(j < ngy - 1, ext[:, 144:152, 0:256], 0.0)
-
-    strip_lane = lax.broadcasted_iota(jnp.int32, (144, 128), 1)
-    for side in range(2):
-        packed = jnp.zeros((144, 128), F32)
-        for v in range(5):
-            if side == 0:
-                moved = pltpu.roll(ext[v, 8:152, 128:256], (8 * v - 120) % 128, 1)
-            else:
-                moved = pltpu.roll(ext[v, 8:152, 0:128], 8 * v, 1) if v else ext[v, 8:152, 0:128]
-            packed = jnp.where((strip_lane >= 8 * v) & (strip_lane < 8 * v + 8), moved, packed)
-        xsend[side] = packed
-
-    relay1()
-
-    def column(to, n):
-        return pltpu.make_async_remote_copy(
-            src_ref=xsend.at[n], dst_ref=xrecv.at[n],
-            send_sem=h_send.at[2 + n], recv_sem=h_recv.at[2 + n],
-            device_id={"gx": to}, device_id_type=MESH,
-        )
-
-    go_right, go_left = column(right, 0), column(left, 1)
-    go_right.start()
-    go_left.start()
-
-    for n in (4, 5, 6):
-        copies[n].wait()
-
-    def combine(c, carry):
-        rows = pl.ds(pl.multiple_of(8 * c, 8), 8)
-        sums = [None] * 6
-        for d in range(ngx):
-            u, v = vg[d, 0, rows, :], vg[d, 1, rows, :]
-            cosine, sine = fxs[d : d + 1, :], fxs[ngx + d : ngx + d + 1, :]
-            for f, value in enumerate((u * u, u * v, v * v)):
-                real, imag = value * cosine, value * sine
-                sums[2 * f] = real if d == 0 else sums[2 * f] + real
-                sums[2 * f + 1] = -imag if d == 0 else sums[2 * f + 1] - imag
-        for f in range(3):
-            zs[f, 0, rows, :] = sums[2 * f]
-            zs[f, 1, rows, :] = sums[2 * f + 1]
-        return carry
-
-    lax.fori_loop(0, 8, combine, 0)
-    w_high, w_low = wxm[0], wxm[1]
-    for f in range(3):
-        pieces = []
-        for real, imag in zip(parts(zs[f, 0]), parts(zs[f, 1])):
-            plain = jnp.concatenate([real, imag], axis=1)
-            turned = jnp.concatenate([imag, -real], axis=1)
-            both = [turned, -plain] if f == 1 else [plain, turned]
-            pieces.append(jnp.concatenate(both, axis=0))
-        high, low = pieces
-        lines = dot_t(w_high, high) + dot_t(w_high, low) + dot_t(w_low, high)
-        for s in range(ns):
-            b3[pl.ds(ns * f + s, ngy, stride=rpm), :] = lines[ngy * s : ngy * s + ngy]
-
-    def offset(m):
-        step = (m + 1) // 2
-        return ngy // 2 + jnp.where(m % 2 == 1, step, -step)
-
-    def send3(k):
-        to = (j + k) % ngy
-        return pltpu.make_async_remote_copy(
-            src_ref=b3.at[pl.ds(pl.multiple_of(to * rpm, 8), rpm), :], dst_ref=r3.at[j],
-            send_sem=y_send.at[k], recv_sem=y_recv.at[j],
-            device_id={"gy": to}, device_id_type=MESH,
-        )
-
-    def recv3(d):
-        return pltpu.make_async_remote_copy(
-            src_ref=r3.at[d], dst_ref=r3.at[d], send_sem=y_send.at[0], recv_sem=y_recv.at[d],
-            device_id={"gy": d}, device_id_type=MESH,
-        )
-
-    def go3(m, carry):
-        send3(offset(m)).start()
-        return carry
-
-    lax.fori_loop(0, ngy - 1, go3, 0)
-    r3[j] = b3[pl.ds(pl.multiple_of(j * rpm, 8), rpm), :]
-
     go_right.wait()
     go_left.wait()
     for v in range(5):
@@ -487,16 +494,6 @@
         return carry
 
     lax.fori_loop(0, 18, stage_one, 0)
-
-    def stage_two(c, carry):
-        at = pl.multiple_of(16 + 8 * c, 8)
-        here = pl.ds(at, 8)
-        open_cells = ext[4, here, 0:256]
-        for v, (value, rate) in enumerate(rates(mid, at, 8)):
-            adv[v, here, :] = open_cells * (adv[v, here, :] - 0.25 * rate[:, 0:256])
-        return carry
-
-    lax.fori_loop(0, 16, stage_two, 0)
 
     def got3(k, carry):
         recv3((j + k) % ngy).wait_recv()
@@ -569,6 +566,17 @@
 
     lax.fori_loop(0, ngy - 1, go4, 0)
     r4[j] = b4[j]
+
+    def stage_two(c, carry):
+        at = pl.multiple_of(16 + 8 * c, 8)
+        here = pl.ds(at, 8)
+        open_cells = ext[4, here, 0:256]
+        for v, (value, rate) in enumerate(rates(mid, at, 8)):
+            adv[v, here, :] = open_cells * (adv[v, here, :] - 0.25 * rate[:, 0:256])
+        return carry
+
+    lax.fori_loop(0, 16, stage_two, 0)
+
     lax.fori_loop(1, ngy, got4, 0)
     for g in range(ngy):
         s4[2 * ns * g : 2 * ns * g + 2 * ns, :] = r4[g]
@@ -659,7 +667,6 @@
             vmem((5, 160, 384), F32),
             vmem((4, 160, 384), F32),
             vmem((4, 160, 256), F32),
-            vmem((8, 128), F32),
             vmem((2, 144, 128), F32),
             vmem((2, 144, 128), F32),
             vmem((2, 256, 384), BF16),
@@ -684,6 +691,7 @@
             dma((4,)), dma((4,)),
             dma((ngy,)), dma((ngy,)),
             dma((ngx,)), dma((ngx,)),
+            pltpu.SemaphoreType.REGULAR,
         ]
         result = pl.pallas_call(
             functools.partial(kernel, ngx, ngy),
@@ -692,7 +700,7 @@
             out_specs=pl.BlockSpec(memory_space=pltpu.VMEM),
             scratch_shapes=scratch,
             compiler_params=pltpu.CompilerParams(
-                collective_id=0, has_side_effects=True, vmem_limit_bytes=40 * 1024 * 1024
+                collective_id=0, has_side_effects=True
             ),
             name="poisson_step",
         )(vel, weights_x, weights_y, ac, wall, fx, wx, twf, yf, twi, yi, dx, cx)

time: 72.1 us -> 58.5 us (0.81)
  local copies, waits for them, and re-layouts: 12.4 us -> 1.67 us
  Pallas kernels: 59.1 us -> 56.6 us
    unnamed x27 -> x1, local copies, waits for them, and re-layouts: 12.4 us -> 1.67 us
    pallas_call x1, Pallas kernels: 59.1 us -> 56.6 us  [shards(): pl.pallas_call(functools.partial(kernel, ngx, ngy), out_shape=jax.ShapeDt...]
where the time goes in v1:
time: 58.5 us; the launch traced here: 58.3 us
  Pallas kernels  56.6 us (97%)
  local copies, waits for them, and re-layouts  1.67 us (3%)
    pallas_call x1, Pallas kernels, shards(): pl.pallas_call(functools.partial(kernel, ngx, ngy), out_shape=jax.ShapeDt...  56.6 us
    unnamed x1, local copies, waits for them, and re-layouts  1.67 us

profile of v1, /device:TPU:1, one launch (start us, length us, event | category | flops | bytes accessed | tf_op | source)
XLA Modules:
  0.0 58.3 jit_solution(6743541955493953147)
XLA Ops:
  0.0 56.6 %poisson_step.1 = bf16[4,128,256]{2,1,0:T(8,128)(2,1)} custom-call(f32[2,64,128]{2,1,0:T(8,128)} %bitcast.9, f32[4,4096]{1,0:T(4,128)} %weights_x.1, f32[4,4096]{1,0:T(4,128)} %weights_y.1, bf16[4,128,256]{2,1,0:T(8,128)(2,1)} %bitcast.7, s32[128,256]{1,0:T(8,128)} %bitcast.8, f32[16,32,128]{2,1,0:T(8,128)} %constant.16.clone.fx, ...), custom_call_target="tpu_custom_call" | custom-call | tf_op jit(solution)/shard_map/poisson_step/pallas_call | solution.py:696
  56.6 1.7 %copy.16 = bf16[4,1,128,256]{3,2,1,0:T(8,128)(2,1)} copy(bf16[4,1,128,256]{3,2,1,0:T(8,128)(2,1)} %bitcast.6) | data formatting | bytes 524288

commit v2 on v1

--- a/solution.py
+++ b/solution.py
@@ -30,14 +30,14 @@
     nx, ny, ns, half = 128 * ngx, 64 * ngy, 64 // ngy, ngy // 2 + 1
     lane = np.arange(128)
     wide = np.arange(256) - 4
-    place = (128 * np.arange(ngx)[:, None] + lane)[None] * np.arange(ngx)[:, None, None]
+    order = np.concatenate([np.arange(0, ngx, 2), np.arange(1, ngx, 2)])
+    place = (128 * order[:, None] + lane)[None] * np.arange(ngx)[:, None, None]
     angle = turn(place, nx)
     fx = np.concatenate([np.cos(angle), np.sin(angle)], axis=1).astype(np.float32)
     angle = turn(np.arange(64)[:, None] * lane[None], 128)
-    plain = np.concatenate([np.cos(angle), np.sin(angle)], axis=1)
-    first = plain.copy()
-    first[0, 128:] = -((-1.0) ** lane)
-    wx = np.stack([two_parts(plain), two_parts(first)])
+    wx = two_parts(np.concatenate([np.cos(angle), np.sin(angle)], axis=1))
+    sums = np.zeros((8, 128), dtype=BF16)
+    sums[0], sums[1] = 1.0, (-1.0) ** lane
     angle = turn(np.arange(half)[:, None] * (lane % 64)[None], ny)
     twf = np.stack([np.cos(angle), np.sin(angle)]).astype(np.float32)
     angle = turn(np.arange(64)[:, None] * np.arange(64)[None], 64)
@@ -59,14 +59,11 @@
     rows = np.zeros((ngy, 2, ns, 512))
     rows[:, 0, :, :256], rows[:, 0, :, 256:] = cosine, sine
     rows[:, 1, :, :256], rows[:, 1, :, 256:] = -sine, cosine
-    packed = rows.copy()
-    packed[0, 0, 0, :256], packed[0, 0, 0, 256:] = 1.0, 0.0
-    packed[0, 1, 0, :256], packed[0, 1, 0, 256:] = (-1.0) ** wide, 0.0
-    dx = np.stack([two_parts(rows.reshape(128, 512)), two_parts(packed.reshape(128, 512))])
-    place = (128 * np.arange(ngx)[:, None] + wide)[:, None, :] * np.arange(ngx)[None, :, None]
+    dx = two_parts(rows.reshape(128, 512))
+    place = (128 * np.arange(ngx)[:, None] + wide)[:, None, :] * order[None, :, None]
     angle = turn(place, nx)
     cx = np.concatenate([np.cos(angle), np.sin(angle)], axis=1).astype(np.float32)
-    return fx, wx, twf, yf, twi, yi, dx, cx
+    return fx, wx, sums, twf, yf, twi, yi, dx, cx
 
 
 def rfft(values):
@@ -189,15 +186,15 @@
 
 def kernel(
     ngx, ngy,
-    vel, weights_x, weights_y, ac, wall, fx, wx, twf, yf, twi, yi, dx, cx,
+    vel, weights_x, weights_y, ac, wall, fx, wx, sums, twf, yf, twi, yi, dx, cx,
     out,
-    vg, acs, wls, wxs, wys, fxs, wxm, twfs, yfs, twis, yis, dxs, cxs,
+    vg, acs, wls, wxs, wys, fxs, wxm, sms, twfs, yfs, twis, yis, dxs, cxs,
     ext, mid, adv, xsend, xrecv, ax, ay, k1, k2,
-    zs, b3, r3, gs, ps, us, b4, r4, s4, sb, sg, qs,
-    loc, x_send, x_recv, y_send, y_recv, h_send, h_recv, v_send, v_recv, w_send, w_recv, token,
+    zs, b2, b3, r3, gs, ps, us, b4, r4, s4, sb, sg, pacc, qs, es, ob,
+    loc, x_send, x_recv, y_send, y_recv, h_send, h_recv, v_send, v_recv, w_send, w_recv, e_send, e_recv, o_sem, token,
 ):
     ns, half = 64 // ngy, ngy // 2 + 1
-    rpm = max(8, 3 * ns)
+    rpm = 2 * ns
     i, j = lax.axis_index("gx"), lax.axis_index("gy")
     partner = i + 1 - 2 * (i % 2)
     right, left = (i + 1) % ngx, (i + ngx - 1) % ngx
@@ -223,10 +220,11 @@
     pl.semaphore_signal(barrier, inc=1, device_id={"gx": right}, device_id_type=MESH)
     pl.semaphore_signal(barrier, inc=1, device_id={"gx": left}, device_id_type=MESH)
 
-    first = jnp.where(i == 0, 1, 0)
+    parity = i % 2
+    place = parity * chips + i // 2
     sources = [
-        (ac, acs), (wall, wls), (weights_x, wxs), (weights_y, wys), (vel, vg.at[i]),
-        (fx.at[i], fxs), (wx.at[first], wxm), (twf, twfs), (yf, yfs), (twi, twis), (yi, yis),
+        (ac, acs), (wall, wls), (weights_x, wxs), (weights_y, wys), (vel, vg.at[place]),
+        (fx.at[i], fxs), (wx, wxm), (sums, sms), (twf, twfs), (yf, yfs), (twi, twis), (yi, yis),
         (dx, dxs), (cx.at[i], cxs),
     ]
     copies = [pltpu.make_async_copy(a, b, loc.at[n]) for n, (a, b) in enumerate(sources)]
@@ -235,10 +233,15 @@
 
     pl.semaphore_wait(barrier, 2 * near + chips - 1 + 2)
 
+    def slot_of(k):
+        return (k % 2) * chips + k // 2
+
     def gather(source, own, slots, send, recv):
+        mine = slot_of(own)
+
         def direct(k):
             return pltpu.make_async_remote_copy(
-                src_ref=source, dst_ref=slots.at[own], send_sem=send.at[k], recv_sem=recv.at[own],
+                src_ref=source, dst_ref=slots.at[mine], send_sem=send.at[k], recv_sem=recv.at[mine],
                 device_id={"gx": (own + 2 * k) % ngx}, device_id_type=MESH,
             )
 
@@ -260,39 +263,39 @@
                 return carry
 
             lax.fori_loop(1, chips, go, 0)
-            to_partner(source, own, 0).start()
+            to_partner(source, mine, 0).start()
 
         def relay():
             def step(k, carry):
-                at = (own + ngx - 2 * k) % ngx
+                at = slot_of((own + ngx - 2 * k) % ngx)
                 arrived(at)
                 to_partner(slots.at[at], at, chips - 1 + k).start()
                 return carry
 
             lax.fori_loop(1, chips, step, 0)
 
-            def rest(k, carry):
-                arrived((partner + ngx - 2 * k) % ngx)
+        def rest():
+            def step(k, carry):
+                arrived(slot_of((partner + ngx - 2 * k) % ngx))
                 return carry
 
-            lax.fori_loop(0, chips, rest, 0)
+            lax.fori_loop(0, chips, step, 0)
 
         def finish():
             def step(k, carry):
                 direct(k).wait_send()
-                to_partner(slots.at[own], own, chips - 1 + k).wait_send()
+                to_partner(slots.at[mine], mine, chips - 1 + k).wait_send()
                 return carry
 
             lax.fori_loop(1, chips, step, 0)
-            to_partner(source, own, 0).wait_send()
-
-        return start, relay, finish
-
-    start1, relay1, finish1 = gather(vel, i, vg, x_send, x_recv)
+            to_partner(source, mine, 0).wait_send()
+
+        return start, relay, rest, finish
+
+    start1, relay1, rest1, finish1 = gather(vel, i, vg, x_send, x_recv)
     start1()
     pl.semaphore_signal(token, inc=1, device_id={"gy": (j + near) % ngy}, device_id_type=MESH)
     pl.semaphore_signal(token, inc=1, device_id={"gy": (j + ngy - near) % ngy}, device_id_type=MESH)
-    b3[...] = jnp.zeros(b3.shape, F32)
     ext[:, 0:8, :] = jnp.zeros((5, 8, 384), F32)
     ext[:, 152:160, :] = jnp.zeros((5, 8, 384), F32)
     copies[0].wait()
@@ -314,30 +317,37 @@
     go_down.start()
     go_up.start()
     relay1()
-
-    for n in (4, 5, 6):
+    for n in (4, 5, 6, 7):
         copies[n].wait()
 
-    def combine(c, carry):
-        rows = pl.ds(pl.multiple_of(8 * c, 8), 8)
-        sums = [None] * 6
-        for d in range(ngx):
-            u, v = vg[d, 0, rows, :], vg[d, 1, rows, :]
-            cosine, sine = fxs[d : d + 1, :], fxs[ngx + d : ngx + d + 1, :]
-            for f, value in enumerate((u * u, u * v, v * v)):
-                real, imag = value * cosine, value * sine
-                sums[2 * f] = real if d == 0 else sums[2 * f] + real
-                sums[2 * f + 1] = -imag if d == 0 else sums[2 * f + 1] - imag
-        for f in range(3):
-            zs[f, 0, rows, :] = sums[2 * f]
-            zs[f, 1, rows, :] = sums[2 * f + 1]
-        return carry
-
-    lax.fori_loop(0, 8, combine, 0)
+    def combine(half_at, begin):
+        def step(c, carry):
+            rows = pl.ds(pl.multiple_of(8 * c, 8), 8)
+            total = [None] * 5 if begin else [zs[n, rows, :] for n in range(5)]
+            for m in range(chips):
+                u, v = vg[half_at + m, 0, rows, :], vg[half_at + m, 1, rows, :]
+                cosine = fxs[pl.ds(half_at + m, 1), :]
+                sine = fxs[pl.ds(ngx + half_at + m, 1), :]
+                uu, vv, uv = u * u, v * v, u * v
+                difference = uu - vv
+                terms = (
+                    difference * cosine, -(difference * sine), uv * cosine, -(uv * sine),
+                    0.5 * (uu + vv),
+                )
+                total = [b if a is None else a + b for a, b in zip(total, terms)]
+            for n in range(5):
+                zs[n, rows, :] = total[n]
+            return carry
+
+        lax.fori_loop(0, 8, step, 0)
+
+    combine(parity * chips, True)
+    rest1()
+    combine(chips - parity * chips, False)
     w_high, w_low = wxm[0], wxm[1]
-    for f in range(3):
+    for f in range(2):
         pieces = []
-        for real, imag in zip(parts(zs[f, 0]), parts(zs[f, 1])):
+        for real, imag in zip(parts(zs[2 * f]), parts(zs[2 * f + 1])):
             plain = jnp.concatenate([real, imag], axis=1)
             turned = jnp.concatenate([imag, -real], axis=1)
             both = [turned, -plain] if f == 1 else [plain, turned]
@@ -345,7 +355,20 @@
         high, low = pieces
         lines = dot_t(w_high, high) + dot_t(w_high, low) + dot_t(w_low, high)
         for s in range(ns):
-            b3[pl.ds(ns * f + s, ngy, stride=rpm), :] = lines[ngy * s : ngy * s + ngy]
+            b2[pl.ds(ns * f + s, ngy, stride=rpm), :] = lines[ngy * s : ngy * s + ngy]
+    alternating, plain_sum = [], None
+    for n in (0, 2, 4):
+        high, low = parts(zs[n])
+        row_sums = dot_t(sms[...], high) + dot_t(sms[...], low)
+        if n == 4:
+            plain_sum = row_sums[0:1]
+        else:
+            alternating.append(row_sums[1:2])
+    b2[0:1, 64:128] = jnp.where(i == 0, alternating[0], b2[0:1, 64:128])
+    b2[ns : ns + 1, 0:64] = jnp.where(i == 0, alternating[1], b2[ns : ns + 1, 0:64])
+    b2[ns : ns + 1, 64:128] = jnp.where(i == 0, plain_sum, b2[ns : ns + 1, 64:128])
+    for g in range(ngy):
+        b3[g] = b2[rpm * g : rpm * g + rpm, :]
 
     def offset(m):
         step = (m + 1) // 2
@@ -354,7 +377,7 @@
     def send3(k):
         to = (j + k) % ngy
         return pltpu.make_async_remote_copy(
-            src_ref=b3.at[pl.ds(pl.multiple_of(to * rpm, 8), rpm), :], dst_ref=r3.at[j],
+            src_ref=b3.at[to], dst_ref=r3.at[j],
             send_sem=y_send.at[k], recv_sem=y_recv.at[j],
             device_id={"gy": to}, device_id_type=MESH,
         )
@@ -371,7 +394,7 @@
 
     pl.semaphore_wait(token, 2)
     lax.fori_loop(0, ngy - 1, go3, 0)
-    r3[j] = b3[pl.ds(pl.multiple_of(j * rpm, 8), rpm), :]
+    r3[j] = b3[j]
 
     go_down.wait()
     go_up.wait()
@@ -413,7 +436,7 @@
         wave_y = jnp.where(index >= 32 * ngy, index - 64 * ngy, index).astype(F32)
         xx, yy = wave_x * wave_x, wave_y * wave_y
         inverse = -1.0 / jnp.maximum(xx + yy, 1.0)
-        k1[q] = jnp.where(field == 0, xx * inverse, jnp.where(field == 2, yy * inverse, 0.0))
+        k1[q] = jnp.where(field == 0, 0.5 * (xx - yy) * inverse, 0.0)
         cross = (field == 1) & jnp.logical_not(is_packed) & (index != 32 * ngy)
         k2[q] = jnp.where(cross, 2.0 * wave_x * wave_y * inverse, 0.0)
         return carry
@@ -495,11 +518,30 @@
 
     lax.fori_loop(0, 18, stage_one, 0)
 
+    energies = []
+    for block in (left, i, right):
+        u, v = vg[slot_of(block), 0], vg[slot_of(block), 1]
+        energies.append(pltpu.roll(0.5 * (u * u + v * v), 4, 1))
+    edge = lax.broadcasted_iota(jnp.int32, (64, 128), 1) < 4
+    es[8:72, 0:128] = jnp.where(edge, energies[0], energies[1])
+    es[8:72, 128:256] = jnp.where(edge, energies[1], energies[2])
+
+    def border(to, rows_from, rows_to, n):
+        return pltpu.make_async_remote_copy(
+            src_ref=es.at[pl.ds(rows_from, 8), :], dst_ref=es.at[pl.ds(rows_to, 8), :],
+            send_sem=e_send.at[n], recv_sem=e_recv.at[n],
+            device_id={"gy": to}, device_id_type=MESH,
+        )
+
+    border_down, border_up = border(down, 64, 0, 0), border(up, 8, 72, 1)
+    border_down.start()
+    border_up.start()
+
     def got3(k, carry):
         recv3((j + k) % ngy).wait_recv()
         return carry
 
-    for n in range(7, 13):
+    for n in range(8, 14):
         copies[n].wait()
     lax.fori_loop(1, ngy, got3, 0)
 
@@ -514,17 +556,18 @@
             gs[rows, 0:128] = real * cosine + imag * sine
             gs[rows, 128:256] = imag * cosine - real * sine
     gs[...] = dot3(parts(gs[...]), (yfs[0], yfs[1]))
-    corner = (row == ns) & (lane == 96) & (i == 0) & (j == 0)
+    origin = (row == ns) & (i == 0) & (j == 0)
+    corner = jnp.where(origin & (lane == 0), 1.0, jnp.where(origin & (lane == 96), -1.0, 0.0))
     row_lane = lax.broadcasted_iota(jnp.int32, (ns, 128), 1)
     for q in range(half):
         real, imag = gs[rpm * q : rpm * q + rpm, 0:128], gs[rpm * q : rpm * q + rpm, 128:256]
         total_real = k1[q] * real - k2[q] * imag
         total_imag = k1[q] * imag + k2[q] * real
         if q == 0:
-            total_real = total_real - jnp.where(corner, pltpu.roll(real, 64, 1), 0.0)
-            total_imag = total_imag - jnp.where(corner, pltpu.roll(imag, 64, 1), 0.0)
+            total_real = total_real + corner * pltpu.roll(real, 64, 1)
+            total_imag = total_imag + corner * pltpu.roll(imag, 64, 1)
         for n, total in enumerate((total_real, total_imag)):
-            value = total[0:ns] + total[ns : 2 * ns] + total[2 * ns : 3 * ns]
+            value = total[0:ns] + total[ns : 2 * ns]
             lanes = slice(128 * n, 128 * n + 128)
             at = 2 * ns * q
             ps[at : at + ns, lanes] = jnp.where(row_lane < 64, value, 0.0)
@@ -576,25 +619,40 @@
         return carry
 
     lax.fori_loop(0, 16, stage_two, 0)
+    ob[0] = adv[0, 16:144, :].astype(BF16)
+    out_first = pltpu.make_async_copy(ob.at[0], out.at[0], o_sem.at[0])
+    out_first.start()
+    border_down.wait()
+    border_up.wait()
 
     lax.fori_loop(1, ngy, got4, 0)
     for g in range(ngy):
         s4[2 * ns * g : 2 * ns * g + 2 * ns, :] = r4[g]
     sb[...] = jnp.transpose(s4[...])[0:PX]
-    start2, relay2, finish2 = gather(sb, i, sg, w_send, w_recv)
+    start2, relay2, rest2, finish2 = gather(sb, i, sg, w_send, w_recv)
     start2()
-    sg[i] = sb[...]
+    sg[place] = sb[...]
+    pacc[...] = -es[4 : 4 + PX, :]
     relay2()
 
-    pressure = jnp.zeros((PX, 256), F32)
-    blocks = [(0, 1, 1)] + [(a, min(a + 5, ngx), 0) for a in range(1, ngx, 5)]
-    for begin, end, variant in blocks:
-        lines = sg[begin:end].reshape((end - begin) * PX, 128)
-        mixed = dot3(parts(lines), (dxs[variant, 0], dxs[variant, 1]))
-        for n in range(begin, end):
-            rows = slice((n - begin) * PX, (n - begin + 1) * PX)
-            cosine, sine = cxs[n : n + 1, :], cxs[ngx + n : ngx + n + 1, :]
+    def unfold(half_at):
+        lines = sg[pl.ds(half_at, chips)].reshape(chips * PX, 128)
+        mixed = dot3(parts(lines), (dxs[0], dxs[1]))
+        pressure = pacc[...]
+        for m in range(chips):
+            rows = slice(m * PX, (m + 1) * PX)
+            cosine = cxs[pl.ds(half_at + m, 1), :]
+            sine = cxs[pl.ds(ngx + half_at + m, 1), :]
             pressure = pressure + (mixed[rows, 0:256] * cosine - mixed[rows, 256:512] * sine)
+        pacc[...] = pressure
+
+    unfold(parity * chips)
+    rest2()
+    unfold(chips - parity * chips)
+    wide = lax.broadcasted_iota(jnp.int32, (PX, 256), 1)
+    alternate = jnp.where(wide % 2 == 0, 1.0, -1.0)
+    packed_lines = sg[0]
+    pressure = pacc[...] - packed_lines[:, 0:1] + packed_lines[:, ns : ns + 1] * alternate
 
     along = dot3(parts(pressure), (ax[0], ax[1]))
     along = jnp.concatenate([along, jnp.zeros((128 - PX, 384), F32)], axis=0)
@@ -613,13 +671,21 @@
         quarter = 0.25 * ext[4, here, 0:256]
         change_x = quarter * slope_x(half_source)[:, 0:256]
         change_y = quarter * slope_y(window, 16)[:, 0:256]
-        out[0, there, :] = adv[0, here, :].astype(BF16)
-        out[1, there, :] = (adv[1, here, :] - change_x).astype(BF16)
-        out[2, there, :] = (adv[2, here, :] - change_y).astype(BF16)
-        out[3, there, :] = (adv[3, here, :] + half_source[:, 0:256] - 0.3 * change_x).astype(BF16)
-        return carry
-
-    lax.fori_loop(0, 8, last, 0)
+        ob[1, there, :] = (adv[1, here, :] - change_x).astype(BF16)
+        ob[2, there, :] = (adv[2, here, :] - change_y).astype(BF16)
+        ob[3, there, :] = (adv[3, here, :] + half_source[:, 0:256] - 0.3 * change_x).astype(BF16)
+        return carry
+
+    outs = [out_first]
+    for n in range(2):
+        lax.fori_loop(4 * n, 4 * n + 4, last, 0)
+        rows = pl.ds(64 * n, 64)
+        outs.append(
+            pltpu.make_async_copy(ob.at[pl.ds(1, 3), rows], out.at[pl.ds(1, 3), rows], o_sem.at[1 + n])
+        )
+        outs[-1].start()
+    for copy in outs:
+        copy.wait()
 
     finish1()
     finish2()
@@ -639,14 +705,14 @@
 def solution(mesh):
     ngx, ngy = mesh.shape["gx"], mesh.shape["gy"]
     ns, half = 64 // ngy, ngy // 2 + 1
-    rpm = max(8, 3 * ns)
+    rpm = 2 * ns
     consts = tables(ngx, ngy)
 
     def shards(velocity, weights_x, weights_y, acoustic, wall_mask):
         vel = velocity.reshape(2, 64, 128)
         ac = acoustic.reshape(4, 128, 256)
         wall = wall_mask.reshape(128, 256)
-        fx, wx, twf, yf, twi, yi, dx, cx = [jnp.asarray(c) for c in consts]
+        fx, wx, sums, twf, yf, twi, yi, dx, cx = [jnp.asarray(c) for c in consts]
         anywhere = pl.BlockSpec(memory_space=pl.ANY)
         vmem = pltpu.VMEM
         dma = pltpu.SemaphoreType.DMA
@@ -657,7 +723,8 @@
             vmem((4, 256 * ngx), F32),
             vmem((4, 128 * ngy), F32),
             vmem(fx.shape[1:], F32),
-            vmem(wx.shape[1:], BF16),
+            vmem(wx.shape, BF16),
+            vmem(sums.shape, BF16),
             vmem(twf.shape, F32),
             vmem(yf.shape, BF16),
             vmem(twi.shape, F32),
@@ -673,8 +740,9 @@
             vmem((2, 256, 128), BF16),
             vmem((half, rpm, 128), F32),
             vmem((half, rpm, 128), F32),
-            vmem((3, 2, 64, 128), F32),
+            vmem((5, 64, 128), F32),
             vmem((ngy * rpm, 128), F32),
+            vmem((ngy, rpm, 128), F32),
             vmem((ngy, rpm, 128), F32),
             vmem((half * rpm, 256), F32),
             vmem((half * 2 * ns, 256), F32),
@@ -684,26 +752,31 @@
             vmem((128, 128), F32),
             vmem((PX, 128), F32),
             vmem((ngx, PX, 128), F32),
+            vmem((PX, 256), F32),
             vmem((160, 384), F32),
-            dma((13,)),
+            vmem((80, 256), F32),
+            vmem((4, 128, 256), BF16),
+            dma((14,)),
             dma((ngx,)), dma((ngx,)),
             dma((ngy,)), dma((ngy,)),
             dma((4,)), dma((4,)),
             dma((ngy,)), dma((ngy,)),
             dma((ngx,)), dma((ngx,)),
+            dma((2,)), dma((2,)),
+            dma((3,)),
             pltpu.SemaphoreType.REGULAR,
         ]
         result = pl.pallas_call(
             functools.partial(kernel, ngx, ngy),
             out_shape=jax.ShapeDtypeStruct((4, 128, 256), BF16),
-            in_specs=[anywhere] * 13,
-            out_specs=pl.BlockSpec(memory_space=pltpu.VMEM),
+            in_specs=[anywhere] * 14,
+            out_specs=anywhere,
             scratch_shapes=scratch,
             compiler_params=pltpu.CompilerParams(
                 collective_id=0, has_side_effects=True
             ),
             name="poisson_step",
-        )(vel, weights_x, weights_y, ac, wall, fx, wx, twf, yf, twi, yi, dx, cx)
+        )(vel, weights_x, weights_y, ac, wall, fx, wx, sums, twf, yf, twi, yi, dx, cx)
         return result.reshape(4, 1, 128, 256)
 
     in_specs = (P(None, None, "gy", "gx"), P(), P(), P(None, None, "gy", "gx"), P(None, "gy", "gx"))

time: 58.5 us -> 57.2 us (0.978)
  Pallas kernels: 56.6 us -> 55.3 us
    pallas_call x1, Pallas kernels: 56.6 us -> 55.3 us  [shards(): pl.pallas_call(functools.partial(kernel, ngx, ngy), out_shape=jax.ShapeDt...]
where the time goes in v2:
time: 57.2 us; the launch traced here: 57 us
  Pallas kernels  55.3 us (97%)
  local copies, waits for them, and re-layouts  1.67 us (3%)
    pallas_call x1, Pallas kernels, shards(): pl.pallas_call(functools.partial(kernel, ngx, ngy), out_shape=jax.ShapeDt...  55.3 us
    unnamed x1, local copies, waits for them, and re-layouts  1.67 us

profile of v2, /device:TPU:1, one launch (start us, length us, event | category | flops | bytes accessed | tf_op | source)
XLA Modules:
  0.0 57.0 jit_solution(16090481047551649067)
XLA Ops:
  0.0 55.3 %poisson_step.1 = bf16[4,128,256]{2,1,0:T(8,128)(2,1)} custom-call(f32[2,64,128]{2,1,0:T(8,128)} %bitcast.9, f32[4,4096]{1,0:T(4,128)} %weights_x.1, f32[4,4096]{1,0:T(4,128)} %weights_y.1, bf16[4,128,256]{2,1,0:T(8,128)(2,1)} %bitcast.7, s32[128,256]{1,0:T(8,128)} %bitcast.8, f32[16,32,128]{2,1,0:T(8,128)} %constant.18.clone.fx, ...), custom_call_target="tpu_custom_call" | custom-call | tf_op jit(solution)/shard_map/poisson_step/pallas_call | solution.py:769
  55.3 1.7 %copy.17 = bf16[4,1,128,256]{3,2,1,0:T(8,128)(2,1)} copy(bf16[4,1,128,256]{3,2,1,0:T(8,128)(2,1)} %bitcast.6) | data formatting | bytes 524288
